TPU v7x, 256 devices: a whole 4x4x8 slice. The times are simulated.
256 devices in a mesh: req: 32 (over z_lo, x, y), tp: 8 (over z_hi, core).
Axes of the slice: x: 4, y: 4, z: 8 (z_hi: 4, z_lo: 2; z = z_hi * 2 + z_lo), core: 2. Of those that a mesh axis runs over, the one named last changes fastest.
Arguments:
- queries: bfloat16 [32768, 5120], P('req', 'tp')
- keys: bfloat16 [32768, 5120], P('req', 'tp')
- values: bfloat16 [32768, 5120], P('req', 'tp'), may hold values from -6 to 6
- cross_queries: bfloat16 [32768, 5120], P('req', 'tp')
- text_kv: bfloat16 [1024, 2, 5120], P(('req', 'tp'))
- segment_ids: int32 [32, 1024], P('req'), may hold values from 0 to 5, never falling along the last dimension, each value on 1 to 682 neighbouring positions
- prompt_of: int32 [32], P('req'), may hold values from 0 to 1
- page_owner: int32 [2048, 1], P('req'), may hold values from 0 to 31; in each aligned block of 64 rows (0 to 63, 64 to 127, ...) at most 3 rows name the same one
Outputs:
- self_out: bfloat16 [32768, 5120], P('req', 'tp')
- cross_out: bfloat16 [32768, 5120], P('req', 'tp')
- cache: bfloat16 [49152, 2, 5120], P('req', None, 'tp')
Inputs may be any that keep to these rules, and one draw needn't show every extreme that they name: `page_owner`: among the pages of one stream (an aligned block of 64 rows), no device index appears more than 3 times; in some streams one appears exactly 3 times.
All inputs are finite; a program needn't handle non-finite values.
Results may differ from a plain program's by a relative error of at most 0.003.
The roundings to bfloat16 on the way count: a program that leaves them out, or rounds other values in their place, can miss the bound.
Values may be sent and summed in bfloat16 or wider, within the bound.
A program may use at most 128 MiB of HBM per device.

v0:
```python
import math
import jax
import jax.numpy as jnp
from jax import lax
from jax.sharding import PartitionSpec as P

HEADS = 40
HEAD = 128
TEXT = 512
PAGE = 16
EPSILON = 1e-06
NEGATIVE = -1e30


def square_sums(block):
    wide = block.astype(jnp.float32)
    return jnp.sum(wide * wide, axis=1)


def scaled_rows(block, totals, width):
    factor = lax.rsqrt(totals / width + EPSILON)
    return (block.astype(jnp.float32) * factor[:, None]).astype(jnp.bfloat16)


def empty_state(heads, count, depth):
    return (
        jnp.full((heads, count), NEGATIVE, jnp.float32),
        jnp.zeros((heads, count), jnp.float32),
        jnp.zeros((heads, count, depth), jnp.float32),
    )


def blend(state, scores, allowed, value_part):
    running_max, running_sum, accum = state
    masked = jnp.where(allowed, scores, NEGATIVE)
    new_max = jnp.maximum(running_max, jnp.max(masked, axis=2))
    weights = jnp.where(allowed, jnp.exp(masked - new_max[:, :, None]), 0.0)
    new_sum = jnp.sum(weights, axis=2)
    product = jnp.einsum(
        "hqk,khe->hqe", weights.astype(jnp.bfloat16), value_part, preferred_element_type=jnp.float32
    )
    return (new_max, new_sum, product)


def finish(state):
    return state[2] / state[1][:, :, None]


def attend_block(state, query_part, query_seg, key_part, value_part, key_seg, scale):
    scores = (
        jnp.einsum("qhe,khe->hqk", query_part, key_part, preferred_element_type=jnp.float32) * scale
    )
    allowed = (query_seg[:, None] == key_seg[None, :])[None]
    return blend(state, scores, allowed, value_part)


def self_attention(query_heads, key_heads, value_heads, segments):
    length, heads, depth = query_heads.shape
    block = math.gcd(length, 512)
    scale = depth ** (-0.5)
    results = []
    for query_start in range(0, length, block):
        query_part = query_heads[query_start : query_start + block]
        query_seg = segments[query_start : query_start + block]
        state = empty_state(heads, block, depth)
        state = attend_block(state, query_part, query_seg, key_heads, value_heads, segments, scale)
        results.append(finish(state))
    joined = jnp.concatenate(results, axis=1)
    return joined.transpose(1, 0, 2).reshape(length, heads * depth).astype(jnp.bfloat16)


def cross_attention(cross_heads, prompt_rows):
    length, heads, depth = cross_heads.shape
    count = prompt_rows.shape[0]
    key_part = prompt_rows[:, 0, :].reshape(count, heads, depth)
    value_part = prompt_rows[:, 1, :].reshape(count, heads, depth)
    block = math.gcd(length, 512)
    scale = depth ** (-0.5)
    everywhere = jnp.ones((1, 1, count), dtype=jnp.bool_)
    results = []
    for query_start in range(0, length, block):
        query_part = cross_heads[query_start : query_start + block]
        scores = (
            jnp.einsum("qhe,khe->hqk", query_part, key_part, preferred_element_type=jnp.float32)
            * scale
        )
        state = blend(empty_state(heads, block, depth), scores, everywhere, value_part)
        results.append(finish(state))
    joined = jnp.concatenate(results, axis=1)
    return joined.transpose(1, 0, 2).reshape(length, heads * depth).astype(jnp.bfloat16)


def per_device(queries, keys, values, cross_queries, text_kv, segment_ids, prompt_of, page_owner):
    width = HEADS * HEAD
    stream = queries.shape[0]
    width_dev = queries.shape[1]
    heads_dev = width_dev // HEAD
    query_total, key_total, cross_total = lax.psum(
        (square_sums(queries), square_sums(keys), square_sums(cross_queries)), "tp"
    )
    query_hat = scaled_rows(queries, query_total, width)
    key_hat = scaled_rows(keys, key_total, width)
    cross_hat = scaled_rows(cross_queries, cross_total, width)
    text_keys = text_kv[:, 0, :]
    text_hat = scaled_rows(text_keys, square_sums(text_keys), width)
    text_ready = jnp.stack([text_hat, text_kv[:, 1, :]], axis=1)
    nreq = lax.axis_size("req")
    pages = stream // PAGE
    capacity = max(2, (3 * pages + 2 * nreq - 1) // (2 * nreq))
    owners = page_owner[:, 0]
    same_owner = owners[:, None] == owners[None, :]
    before = lax.broadcasted_iota(jnp.int32, (pages, pages), 1) < lax.broadcasted_iota(
        jnp.int32, (pages, pages), 0
    )
    rank = jnp.sum(jnp.where(jnp.logical_and(same_owner, before), 1, 0), axis=1).astype(jnp.int32)
    slot_index = owners * capacity + rank
    picker = (
        lax.broadcasted_iota(jnp.int32, (nreq * capacity, pages), 0) == slot_index[None, :]
    ).astype(jnp.bfloat16)
    page_data = jnp.stack([key_hat, values], axis=1).reshape(pages, PAGE * 2 * width_dev)
    outgoing = jnp.dot(picker, page_data, preferred_element_type=jnp.float32).astype(jnp.bfloat16)
    outgoing = outgoing.reshape(nreq * capacity * PAGE, 2, width_dev)
    cache = lax.all_to_all(outgoing, "req", split_axis=0, concat_axis=0, tiled=True)
    query_heads = query_hat.reshape(stream, heads_dev, HEAD)
    key_heads = key_hat.reshape(stream, heads_dev, HEAD)
    value_heads = values.reshape(stream, heads_dev, HEAD)
    self_out = self_attention(query_heads, key_heads, value_heads, segment_ids[0])
    cross_heads = cross_hat.reshape(stream, heads_dev, HEAD)
    prompt_start = prompt_of[0] * TEXT
    gathered = lax.all_gather(text_ready, ("req", "tp"), axis=0, tiled=True)
    prompt_rows = lax.dynamic_slice_in_dim(gathered, prompt_start, TEXT, 0)
    head_start = lax.axis_index("tp") * width_dev
    prompt_rows = lax.dynamic_slice_in_dim(prompt_rows, head_start, width_dev, 2)
    cross_out = cross_attention(cross_heads, prompt_rows)
    return (self_out, cross_out, cache)


def solution(mesh):
    placed = (
        P("req", "tp"),
        P("req", "tp"),
        P("req", "tp"),
        P("req", "tp"),
        P(("req", "tp"), None, None),
        P("req", None),
        P("req"),
        P("req", None),
    )
    return jax.shard_map(
        per_device,
        mesh=mesh,
        in_specs=placed,
        out_specs=(P("req", "tp"), P("req", "tp"), P("req", None, "tp")),
        check_vma=False,
    )
```

profile of v0, /device:TPU:64, one launch (start us, length us, event | category | flops | bytes accessed | tf_op | source)
XLA Modules:
  0.0 517.8 jit_solution(12269761902777181673)
XLA Ops:
  7.2 0.0 copy-start.3
  7.2 0.0 all-gather.2.cloned.1.call-start
  7.2 1.2 fusion.52
  8.4 0.2 fusion.38
  8.6 0.1 fusion.39
  8.7 0.1 pad_maximum_fusion.1
  8.7 0.7 copy.86
  9.4 0.0 all-gather.2.cloned.1.call-update
  9.5 1.6 copy.74
  11.1 0.0 copy-done.3
  11.1 1.5 copy.73
  12.6 1.6 copy.83
  14.2 2.4 copy.77
  16.6 0.3 fusion.18
  16.9 1.6 fusion.16
  18.5 0.3 fusion.20
  18.8 28.2 %all-reduce = (f32[1024]{0:T(1024)S(1)}, f32[1024]{0:T(1024)S(1)}, f32[1024]{0:T(1024)S(1)}) all-reduce(f32[1024]{0:T(1024)S(1)} %fusion.16, f32[1024]{0:T(1024)S(1)} %fusion.18, f32[1024]{0:T(1024)S(1)} %fusion.20), channel_id=1, replica_groups=mesh['req'=32,'tp'=8] {'tp'}, use_global_device_ids=true, to_apply=%region_1.0 | all-reduce | flops 3072 | bytes 24576 | tf_op jit(solution)/shard_map/psum | solution.py:98
  47.1 0.0 copy-start.1
  47.1 0.3 fusion.67
  47.4 1.0 copy-done.1
  48.4 1.7 pad_maximum_fusion
  50.1 7.5 %copy.98 = bf16[1024,2,640]{2,1,0:T(2,128)(2,1)} copy(bf16[1024,2,640]{0,2,1:T(8,128)(2,1)} %pad_maximum_fusion) | data formatting | bytes 5242880 | tf_op jit(solution)/shard_map/stack | solution.py:120
  57.6 0.0 copy-start.5
  57.6 5.0 reshape.137
  62.6 0.0 copy-done.5
  62.6 0.2 select_reduce_fusion
  62.8 4.9 convolution_convert_fusion
  67.6 6.8 %reshape.138 = bf16[1536,2,640]{2,1,0:T(2,128)(2,1)} reshape(bf16[96,20480]{1,0:T(8,128)(2,1)} %convolution_convert_fusion) | data formatting | bytes 7864320 | tf_op jit(solution)/shard_map/reshape | solution.py:122
  74.4 7.9 %all-to-all-start = ((bf16[1536,2,640]{2,1,0:T(2,128)(2,1)}), bf16[1536,2,640]{2,1,0:T(2,128)(2,1)}, u32[]{:S(2)}, u32[]{:S(2)}) async-start(bf16[1536,2,640]{2,1,0:T(2,128)(2,1)} %reshape.138), calls=%async_computation | async-start | bytes 7864320 | tf_op jit(solution)/shard_map/all_to_all | solution.py:123
  82.3 0.0 copy-start.4
  82.4 2.7 fusion.17
  85.7 0.0 copy-done.4
  85.8 1.4 fusion.51
  87.1 0.7 broadcast_compare_fusion.1
  87.8 0.3 fusion.19
  88.1 2.3 fusion
  90.4 2.3 fusion.1
  92.7 0.0 copy-start.2
  92.7 6.9 %fusion.2 = (f32[5,512]{1,0:T(8,128)S(1)}, f32[5,512]{1,0:T(8,128)S(1)}) fusion(f32[5,512,1024]{2,1,0:T(8,128)S(1)} %get-tuple-element.30, f32[5,512]{1,0:T(8,128)S(1)} %broadcast_maximum_fusion.3, pred[512,1024]{1,0:T(8,128)(4,1)S(1)} %get-tuple-element.23, f32[5,512]{1,0:T(8,128)S(1)} %broadcast_maximum_fusion.2, f32[5,512,1024]{2,1,0:T(8,128)S(1)} %get-tuple-element.28, ...), kind=kLoop, calls=%fused_computation.7 | loop fusion | flops 26209280 | bytes 22061056 | tf_op jit(solution)/shard_map/reduce_sum | solution.py:38
  99.7 0.0 copy-done.2
  99.7 3.3 divide_convert_fusion.3
  103.0 3.3 divide_convert_fusion.2
  106.3 0.1 maximum_bitcast_fusion
  106.4 1.4 copy.82
  107.8 2.4 copy.99
  110.3 0.3 fusion.21
  110.6 0.1 fusion.50
  110.7 24.5 %all-to-all-done = bf16[1536,2,640]{2,1,0:T(2,128)(2,1)} async-done(((bf16[1536,2,640]{2,1,0:T(2,128)(2,1)}), bf16[1536,2,640]{2,1,0:T(2,128)(2,1)}, u32[]{:S(2)}, u32[]{:S(2)}) %all-to-all-start) | async-done | bytes 3932192 | tf_op jit(solution)/shard_map/all_to_all | solution.py:123
  135.2 344.2 %all-gather.2.cloned.1.call-done = bf16[1024,2,5120]{2,1,0:T(2,128)(2,1)} async-done(((bf16[4,2,5120]{2,1,0:T(2,128)(2,1)}), bf16[1024,2,5120]{2,1,0:T(2,128)(2,1)}) %all-gather.2.cloned.1.call-update) | async-done | bytes 20971536 | tf_op jit(solution)/shard_map/all_gather | solution.py:130
  479.4 7.7 %constant_dynamic-slice_fusion = (bf16[512,1,640]{2,1,0:T(2,128)(2,1)}, bf16[512,1,640]{2,1,0:T(2,128)(2,1)S(1)}) fusion(bf16[1024,2,5120]{2,1,0:T(2,128)(2,1)} %all-gather.2.cloned.1.call-done, s32[]{:T(128)S(6)} %select_n.37, s32[]{:T(128)S(6)} %select_n.39, s32[]{:T(128)S(6)} %add.45), kind=kLoop, calls=%fused_computation.69 | loop fusion | bytes 2621452 | tf_op jit(solution)/shard_map/slice | solution.py:75
  487.1 2.5 copy.118
  489.7 3.2 multiply_reduce_fusion.1
  492.9 1.0 copy.119
  493.9 0.0 copy-start
  493.9 0.9 multiply_reduce_fusion
  494.8 1.6 copy-done
  496.3 0.9 fusion.12
  497.2 1.6 divide_convert_fusion.1
  498.8 0.9 fusion.14
  499.7 1.6 divide_convert_fusion
  501.3 0.1 maximum_bitcast_fusion.1
  501.4 0.6 copy.96
  502.0 1.4 copy.100
  503.5 7.5 %copy.124 = bf16[1536,2,640]{2,1,0:T(2,128)(2,1)} copy(bf16[1536,2,640]{2,1,0:T(2,128)(2,1)} %all-to-all-done) | data formatting | bytes 7864320
  (11 shorter events, 0.1 us)
Async XLA Ops:
  7.2 3.9 copy-start.3
  7.2 472.2 %all-gather.2.cloned.1.call-start = ((), (), s32[]{:S(2)}) async-start(), calls=%async_computation.1 | async-start | bytes 21053440 | tf_op jit(solution)/shard_map/all_gather | solution.py:130
  47.1 1.3 copy-start.1
  57.6 5.0 copy-start.5
  74.4 60.8 %all-to-all-start = ((bf16[1536,2,640]{2,1,0:T(2,128)(2,1)}), bf16[1536,2,640]{2,1,0:T(2,128)(2,1)}, u32[]{:S(2)}, u32[]{:S(2)}) async-start(bf16[1536,2,640]{2,1,0:T(2,128)(2,1)} %reshape.138), calls=%async_computation | async-start | bytes 7864320 | tf_op jit(solution)/shard_map/all_to_all | solution.py:123
  82.3 3.4 copy-start.4
  92.7 7.0 %copy-start.2 = (bf16[1024,640]{0,1:T(8,128)(2,1)S(1)}, bf16[1024,640]{0,1:T(8,128)(2,1)}, u32[]{:S(2)}) copy-start(bf16[1024,640]{0,1:T(8,128)(2,1)} %copy.77) | copy-start | bytes 3932164
  493.9 2.5 copy-start
Sparse Core Ops, SparseCore 0:
  9.9 469.4 all-gather.1
where the time goes:
time: 519 us; the launch traced here: 518 us
  waiting for transfers between devices  369 us (71%)
  local copies, waits for them, and re-layouts  57 us (11%)
  blocking collectives  28.2 us (5%)
  matrix products  23.3 us (4%)
  other arithmetic  17.7 us (3%)
  between operations  15 us (3%)
  starting transfers between devices  7.92 us (2%)
    all_gather x1, waiting for transfers between devices, per_device(): gathered = lax.all_gather(text_ready, ('req', 'tp'), axis=0, tiled=True)  344 us
    psum x1, blocking collectives, per_device(): lax.psum((square_sums(queries), square_sums(keys), square_sums(cross_quer...  28.2 us
    unnamed x22, local copies, waits for them, and re-layouts  24.6 us
    all_to_all x1, waiting for transfers between devices, per_device(): lax.all_to_all(outgoing, 'req', split_axis=0, concat_axis=0, tiled=True)  24.5 us
  transfers between devices with their start and end apart: 2, of which 2 were waited for; matrix products, arithmetic and copies ran while one was open for 12% of the time, Pallas kernels for 0%

commit v1 on v0

--- a/solution.py
+++ b/solution.py
@@ -127,7 +127,10 @@
     self_out = self_attention(query_heads, key_heads, value_heads, segment_ids[0])
     cross_heads = cross_hat.reshape(stream, heads_dev, HEAD)
     prompt_start = prompt_of[0] * TEXT
-    gathered = lax.all_gather(text_ready, ("req", "tp"), axis=0, tiled=True)
+    gathered = jnp.concatenate(
+        lax.all_to_all(jnp.stack([text_ready] * lax.axis_size(("req", "tp"))), ("req", "tp"), 0, 0),
+        axis=0,
+    )
     prompt_rows = lax.dynamic_slice_in_dim(gathered, prompt_start, TEXT, 0)
     head_start = lax.axis_index("tp") * width_dev
     prompt_rows = lax.dynamic_slice_in_dim(prompt_rows, head_start, width_dev, 2)

time: 519 us -> 644 us (1.24)
  waiting for transfers between devices: 369 us -> 473 us
  starting transfers between devices: 7.92 us -> 29.4 us
  between operations: 15 us -> 1.61 us
  local copies, waits for them, and re-layouts: 57 us -> 66 us
    all_to_all x0 -> x1, waiting for transfers between devices: none -> 426 us  [per_device(): lax.all_to_all(jnp.stack([text_ready] * lax.axis_size(('req', 'tp'))), ('...]
    all_gather x1 -> x0, waiting for transfers between devices: 344 us -> none  [per_device(): gathered = lax.all_gather(text_ready, ('req', 'tp'), axis=0, tiled=True)]
    all_to_all x1, waiting for transfers between devices: 24.5 us -> 46.9 us  [per_device(): lax.all_to_all(outgoing, 'req', split_axis=0, concat_axis=0, tiled=True)]
    all_to_all x0 -> x1, starting transfers between devices: none -> 21.4 us  [per_device(): lax.all_to_all(jnp.stack([text_ready] * lax.axis_size(('req', 'tp'))), ('...]
    another operation x1, local copies, waits for them, and re-layouts: 0.69 us -> 12.6 us  [per_device(): jnp.stack([text_ready] * lax.axis_size(('req', 'tp')))]
    unnamed x22 -> x23, local copies, waits for them, and re-layouts: 24.6 us -> 22.2 us
  transfers between devices with their start and end apart: 2 -> 2, of which waited for: 2 -> 2; matrix products, arithmetic and copies ran while one was open for 12% -> 4% of each run, Pallas kernels for 0% -> 0%
where the time goes in v1:
time: 644 us; the launch traced here: 638 us
  waiting for transfers between devices  473 us (73%)
  local copies, waits for them, and re-layouts  66 us (10%)
  starting transfers between devices  29.4 us (5%)
  blocking collectives  28 us (4%)
  matrix products  24.4 us (4%)
  other arithmetic  15.5 us (2%)
    all_to_all x1, waiting for transfers between devices, per_device(): lax.all_to_all(jnp.stack([text_ready] * lax.axis_size(('req', 'tp'))), ('...  426 us
    all_to_all x1, waiting for transfers between devices, per_device(): lax.all_to_all(outgoing, 'req', split_axis=0, concat_axis=0, tiled=True)  46.9 us
    psum x1, blocking collectives, per_device(): lax.psum((square_sums(queries), square_sums(keys), square_sums(cross_quer...  28 us
    unnamed x23, local copies, waits for them, and re-layouts  22.2 us
    all_to_all x1, starting transfers between devices, per_device(): lax.all_to_all(jnp.stack([text_ready] * lax.axis_size(('req', 'tp'))), ('...  21.4 us
  transfers between devices with their start and end apart: 2, of which 2 were waited for; matrix products, arithmetic and copies ran while one was open for 4% of the time, Pallas kernels for 0%

profile of v1, /device:TPU:64, one launch (start us, length us, event | category | flops | bytes accessed | tf_op | source)
XLA Modules:
  0.0 637.5 jit_solution(2879532188866976282)
XLA Ops:
  0.6 1.6 copy.69
  2.2 0.3 fusion.18
  2.5 1.6 copy.68
  4.2 0.0 copy-start.1
  4.2 1.0 copy-done.1
  5.2 0.3 fusion.16
  5.5 1.6 copy.78
  7.1 0.3 fusion.20
  7.4 28.0 %all-reduce = (f32[1024]{0:T(1024)S(1)}, f32[1024]{0:T(1024)S(1)}, f32[1024]{0:T(1024)S(1)}) all-reduce(f32[1024]{0:T(1024)S(1)} %fusion.16, f32[1024]{0:T(1024)S(1)} %fusion.18, f32[1024]{0:T(1024)S(1)} %fusion.20), channel_id=1, replica_groups=mesh['req'=32,'tp'=8] {'tp'}, use_global_device_ids=true, to_apply=%region_1.0 | all-reduce | flops 3072 | bytes 24576 | tf_op jit(solution)/shard_map/psum | solution.py:98
  35.5 2.4 copy.72
  37.9 0.0 copy-start.2
  37.9 0.3 fusion.64
  38.2 1.0 copy-done.2
  39.2 1.7 pad_maximum_fusion
  40.9 7.5 %copy.91 = bf16[1024,2,640]{2,1,0:T(2,128)(2,1)} copy(bf16[1024,2,640]{0,2,1:T(8,128)(2,1)} %pad_maximum_fusion) | data formatting | bytes 5242880 | tf_op jit(solution)/shard_map/stack | solution.py:120
  48.5 4.9 reshape.143
  53.4 0.0 copy-done.7
  53.4 0.2 select_reduce_fusion
  53.6 4.8 convolution_convert_fusion
  58.4 6.7 %reshape.144 = bf16[1536,2,640]{2,1,0:T(2,128)(2,1)} reshape(bf16[96,20480]{1,0:T(8,128)(2,1)} %convolution_convert_fusion) | data formatting | bytes 7864320 | tf_op jit(solution)/shard_map/reshape | solution.py:122
  65.1 8.0 %all-to-all-start.1 = ((bf16[1536,2,640]{2,1,0:T(2,128)(2,1)}), bf16[1536,2,640]{2,1,0:T(2,128)(2,1)}, u32[]{:S(2)}, u32[]{:S(2)}) async-start(bf16[1536,2,640]{2,1,0:T(2,128)(2,1)} %reshape.144), calls=%async_computation.1 | async-start | bytes 7864320 | tf_op jit(solution)/shard_map/all_to_all | solution.py:123
  73.2 0.0 copy-done.5
  73.2 0.1 slice.53
  73.3 0.2 multiply_reduce_fusion.2
  73.5 0.1 multiply_convert_fusion
  73.6 0.2 pad_maximum_fusion.1
  73.8 46.9 %all-to-all-done.1 = bf16[1536,2,640]{2,1,0:T(2,128)(2,1)} async-done(((bf16[1536,2,640]{2,1,0:T(2,128)(2,1)}), bf16[1536,2,640]{2,1,0:T(2,128)(2,1)}, u32[]{:S(2)}, u32[]{:S(2)}) %all-to-all-start.1) | async-done | bytes 3932192 | tf_op jit(solution)/shard_map/all_to_all | solution.py:123
  120.7 12.6 %stack.11 = bf16[256,4,2,5120]{3,2,1,0:T(2,128)(2,1)} broadcast(bf16[4,2,5120]{2,1,0:T(2,128)(2,1)S(1)} %pad_maximum_fusion.1), dimensions={1,2,3} | broadcast | bytes 21053440 | tf_op jit(solution)/shard_map/stack | solution.py:131
  133.3 21.4 %all-to-all-start = ((bf16[256,4,2,5120]{3,2,1,0:T(2,128)(2,1)}), bf16[256,4,2,5120]{3,2,1,0:T(2,128)(2,1)}, u32[]{:S(2)}, u32[]{:S(2)}) async-start(bf16[256,4,2,5120]{3,2,1,0:T(2,128)(2,1)} %stack.11), calls=%async_computation | async-start | bytes 41943040 | tf_op jit(solution)/shard_map/all_to_all | solution.py:131
  155.3 0.0 copy-done.6
  155.4 1.6 fusion.17
  157.0 0.1 fusion.49
  157.1 0.7 broadcast_compare_fusion.1
  157.8 0.3 fusion.19
  158.1 2.3 fusion
  160.4 2.3 fusion.1
  162.7 0.0 copy-start.3
  162.7 6.9 %fusion.2 = (f32[5,512]{1,0:T(8,128)S(1)}, f32[5,512]{1,0:T(8,128)S(1)}) fusion(f32[5,512,1024]{2,1,0:T(8,128)S(1)} %get-tuple-element.28, f32[5,512]{1,0:T(8,128)S(1)} %broadcast_maximum_fusion.3, pred[512,1024]{1,0:T(8,128)(4,1)S(1)} %get-tuple-element.21, f32[5,512]{1,0:T(8,128)S(1)} %broadcast_maximum_fusion.2, f32[5,512,1024]{2,1,0:T(8,128)S(1)} %get-tuple-element.26, ...), kind=kLoop, calls=%fused_computation.7 | loop fusion | flops 26209280 | bytes 22061056 | tf_op jit(solution)/shard_map/reduce_sum | solution.py:38
  169.7 0.0 copy-done.3
  169.7 3.3 divide_convert_fusion.3
  173.0 3.3 divide_convert_fusion.2
  176.3 0.1 maximum_bitcast_fusion
  176.4 1.4 copy.77
  177.8 2.4 copy.92
  180.2 0.3 fusion.21
  180.6 1.1 fusion.48
  181.7 425.7 %all-to-all-done = bf16[256,4,2,5120]{3,2,1,0:T(2,128)(2,1)} async-done(((bf16[256,4,2,5120]{3,2,1,0:T(2,128)(2,1)}), bf16[256,4,2,5120]{3,2,1,0:T(2,128)(2,1)}, u32[]{:S(2)}, u32[]{:S(2)}) %all-to-all-start) | async-done | bytes 20971552 | tf_op jit(solution)/shard_map/all_to_all | solution.py:131
  607.4 6.7 %constant_dynamic-slice_fusion = (bf16[512,1,640]{2,1,0:T(2,128)(2,1)S(1)}, bf16[512,1,640]{2,1,0:T(2,128)(2,1)S(1)}) fusion(bf16[1024,2,5120]{2,1,0:T(2,128)(2,1)} %bitcast.10, s32[]{:T(128)S(6)} %select_n.37, s32[]{:T(128)S(6)} %select_n.39, s32[]{:T(128)S(6)} %add.45), kind=kLoop, calls=%fused_computation.67 | loop fusion | bytes 2621452 | tf_op jit(solution)/shard_map/slice | solution.py:75
  614.1 1.0 copy.79
  615.1 0.0 copy-start.4
  615.1 4.4 multiply_reduce_fusion.1
  619.5 1.0 copy.82
  620.4 0.0 copy-done.4
  620.4 0.0 copy-start
  620.4 0.9 multiply_reduce_fusion
  621.4 1.6 copy-done
  622.9 0.9 fusion.12
  623.8 1.6 divide_convert_fusion.1
  625.4 0.9 fusion.14
  626.3 1.6 divide_convert_fusion
  627.9 0.1 maximum_bitcast_fusion.1
  628.0 0.6 copy.89
  628.6 1.4 copy.93
  630.0 7.5 %copy.110 = bf16[1536,2,640]{2,1,0:T(2,128)(2,1)} copy(bf16[1536,2,640]{2,1,0:T(2,128)(2,1)} %all-to-all-done.1) | data formatting | bytes 7864320
  (13 shorter events, 0.1 us)
Async XLA Ops:
  4.2 1.1 copy-start.1
  37.9 1.3 copy-start.2
  48.5 4.9 copy-start.7
  65.1 8.0 %copy-start.5 = (bf16[4,2,5120]{2,1,0:T(2,128)(2,1)S(1)}, bf16[4,2,5120]{2,1,0:T(2,128)(2,1)}, u32[]{:S(2)}) copy-start(bf16[4,2,5120]{2,1,0:T(2,128)(2,1)} %param.12) | copy-start | bytes 245764
  65.1 55.6 %all-to-all-start.1 = ((bf16[1536,2,640]{2,1,0:T(2,128)(2,1)}), bf16[1536,2,640]{2,1,0:T(2,128)(2,1)}, u32[]{:S(2)}, u32[]{:S(2)}) async-start(bf16[1536,2,640]{2,1,0:T(2,128)(2,1)} %reshape.144), calls=%async_computation.1 | async-start | bytes 7864320 | tf_op jit(solution)/shard_map/all_to_all | solution.py:123
  133.3 22.0 %copy-start.6 = (s32[1,1024]{1,0:T(1,128)S(1)}, s32[1,1024]{1,0:T(1,128)}, u32[]{:S(2)}) copy-start(s32[1,1024]{1,0:T(1,128)} %param.13) | copy-start | bytes 12292
  133.3 474.1 %all-to-all-start = ((bf16[256,4,2,5120]{3,2,1,0:T(2,128)(2,1)}), bf16[256,4,2,5120]{3,2,1,0:T(2,128)(2,1)}, u32[]{:S(2)}, u32[]{:S(2)}) async-start(bf16[256,4,2,5120]{3,2,1,0:T(2,128)(2,1)} %stack.11), calls=%async_computation | async-start | bytes 41943040 | tf_op jit(solution)/shard_map/all_to_all | solution.py:131
  162.7 7.0 %copy-start.3 = (bf16[1024,640]{0,1:T(8,128)(2,1)S(1)}, bf16[1024,640]{0,1:T(8,128)(2,1)}, u32[]{:S(2)}) copy-start(bf16[1024,640]{0,1:T(8,128)(2,1)} %copy.72) | copy-start | bytes 3932164
  615.1 5.3 copy-start.4
  620.4 2.5 copy-start
